TPU v7x, 32 devices: a whole 2x2x4 slice. The times are simulated.
32 devices in a mesh: gx: 8 (over z, x), gy: 4 (over y, core).
Axes of the slice: x: 2, y: 2, z: 4, core: 2. Of those that a mesh axis runs over, the one named last changes fastest.
Arguments:
- maps: bfloat16 [8, 4, 2048, 2048], P('gx', 'gy'), may hold values from -0.125 to 0.125
- sources: float32 [8, 4, 256, 2048], P('gx', 'gy'), may hold values from -6 to 6
- traces: bfloat16 [8, 4, 256, 2048], P('gx', 'gy'), may hold values from -6 to 6
Outputs:
- outgoing: bfloat16 [8, 4, 256, 2048], P('gx', 'gy')
All inputs are finite; a program needn't handle non-finite values.
Results may differ from a plain program's by a relative error of at most 0.0085.
Values may be sent and summed in bfloat16 or wider, within the bound.
A program may use at most 64 MiB of HBM per device.

v0:
```python
import jax
import jax.numpy as jnp
from jax import lax
from jax.sharding import PartitionSpec as P

TICKS = 8


def from_behind(array, axis, by):
    size = lax.axis_size(axis)
    pairs = [(i, i + by) for i in range(size) if 0 <= i + by < size]
    return lax.ppermute(array, axis, pairs)


def project(state, weights, source, low, width):
    value = jnp.dot(state, weights[:, low : low + width], preferred_element_type=jnp.float32)
    return (value + source[:, low : low + width]).astype(jnp.bfloat16)


def two_faces(state, weights, source, low, face):
    both = project(state, weights, source, low, 2 * face)
    return (both[:, :face], both[:, face:])


def downstream(state, weights, source, face):
    east, north = two_faces(state, weights, source, 2 * face, face)
    west_new = from_behind(east, "gx", 1)
    south_new = from_behind(north, "gy", 1)
    return jnp.concatenate([west_new, south_new, state[:, 2 * face :]], axis=1)


def upstream(state, weights, source, face):
    west, south = two_faces(state, weights, source, 0, face)
    east_new = from_behind(west, "gx", -1)
    north_new = from_behind(south, "gy", -1)
    return jnp.concatenate([state[:, : 2 * face], east_new, north_new], axis=1)


def advance(state, weights, source, face, going_down):
    if going_down:
        return downstream(state, weights, source, face)
    return upstream(state, weights, source, face)


def on_device(maps, sources, traces):
    weights = maps[0, 0]
    source = sources[0, 0]
    state = traces[0, 0]
    face = weights.shape[0] // 4
    for tick in range(TICKS - 1):
        going_down = tick < TICKS // 2
        state = advance(state, weights, source, face, going_down)
    result = project(state, weights, source, 0, 4 * face)
    return result[None, None]


def solution(mesh):
    return jax.shard_map(
        on_device,
        mesh=mesh,
        in_specs=(P("gx", "gy", None, None), P("gx", "gy", None, None), P("gx", "gy", None, None)),
        out_specs=P("gx", "gy", None, None),
        check_vma=False,
    )
```

profile of v0, /device:TPU:17, one launch (start us, length us, event | category | flops | bytes accessed | tf_op | source)
XLA Modules:
  0.0 93.2 jit_solution(6847394353121672088)
XLA Ops:
  0.0 0.0 copy-start
  0.0 0.0 copy-start.1
  0.0 4.2 %fusion.55 = bf16[256,1024]{1,0:T(8,128)(2,1)S(1)} fusion(bf16[2048,2048]{1,0:T(8,128)(2,1)} %bitcast.11, f32[256,2048]{1,0:T(8,128)} %bitcast.18, bf16[1,1,256,2048]{3,2,1,0:T(8,128)(2,1)} %param.5), kind=kOutput, calls=%fused_computation.34 | convolution fusion | flops 1074266112 | bytes 6815744 | tf_op jit(solution)/shard_map/dot_general | solution.py:16
  4.3 3.3 %collective-permute-start = (bf16[256,512]{1,0:T(8,128)(2,1)S(1)}, bf16[256,512]{1,0:T(8,128)(2,1)S(1)}, u32[]{:S(2)}, u32[]{:S(2)}) collective-permute-start(bf16[256,512]{1,0:T(8,128)(2,1)S(1)} %get-tuple-element.17), channel_id=1, source_target_pairs={{0,4},{4,8},{8,12},{12,16},{16,20},{20,24},{24,28},{1,5},{5,9},{9,... | collective-permute-start | bytes 786440 | tf_op jit(solution)/shard_map/ppermute | solution.py:12
  7.5 4.0 %collective-permute-start.1 = (bf16[256,512]{1,0:T(8,128)(2,1)S(1)}, bf16[256,512]{1,0:T(8,128)(2,1)S(1)}, u32[]{:S(2)}, u32[]{:S(2)}) collective-permute-start(bf16[256,512]{1,0:T(8,128)(2,1)S(1)} %get-tuple-element.18), channel_id=1, source_target_pairs={{0,1},{1,2},{2,3},{4,5},{5,6},{6,7},{8,9},{9,10},{10,11},{12,13},{... | collective-permute-start | bytes 786440 | tf_op jit(solution)/shard_map/ppermute | solution.py:12
  11.5 0.0 copy-done
  11.6 0.0 copy-start.2
  11.6 2.8 %collective-permute-done = bf16[256,512]{1,0:T(8,128)(2,1)S(1)} collective-permute-done((bf16[256,512]{1,0:T(8,128)(2,1)S(1)}, bf16[256,512]{1,0:T(8,128)(2,1)S(1)}, u32[]{:S(2)}, u32[]{:S(2)}) %collective-permute-start) | collective-permute-done | bytes 262176 | tf_op jit(solution)/shard_map/ppermute | solution.py:12
  14.4 0.4 collective-permute-done.1
  14.8 0.0 copy-done.1
  14.8 2.5 %fusion.52 = bf16[256,1024]{1,0:T(8,128)(2,1)S(1)} fusion(bf16[2048,2048]{1,0:T(8,128)(2,1)S(1)} %bitcast.12, bf16[256,1024]{1,0:T(8,128)(2,1)S(1)} %slice.92, bf16[256,512]{1,0:T(8,128)(2,1)S(1)} %collective-permute-done.1, bf16[256,512]{1,0:T(8,128)(2,1)S(1)} %collective-permute-done, f32[256,2048]{1,0:T(8,128)} %bitcast.19), kind=kOutput, calls=%fused_computation.33 | convolution fusion | flops 1077411840 | bytes 6815744 | tf_op jit(solution)/shard_map/dot_general | solution.py:16
  17.4 3.2 %collective-permute-start.2 = (bf16[256,512]{1,0:T(8,128)(2,1)S(1)}, bf16[256,512]{1,0:T(8,128)(2,1)S(1)}, u32[]{:S(2)}, u32[]{:S(2)}) collective-permute-start(bf16[256,512]{1,0:T(8,128)(2,1)S(1)} %get-tuple-element.15), channel_id=1, source_target_pairs={{0,4},{4,8},{8,12},{12,16},{16,20},{20,24},{24,28},{1,5},{5,9},{9,... | collective-permute-start | bytes 786440 | tf_op jit(solution)/shard_map/ppermute | solution.py:12
  20.5 4.7 %collective-permute-start.3 = (bf16[256,512]{1,0:T(8,128)(2,1)S(1)}, bf16[256,512]{1,0:T(8,128)(2,1)S(1)}, u32[]{:S(2)}, u32[]{:S(2)}) collective-permute-start(bf16[256,512]{1,0:T(8,128)(2,1)S(1)} %get-tuple-element.16), channel_id=1, source_target_pairs={{0,1},{1,2},{2,3},{4,5},{5,6},{6,7},{8,9},{9,10},{10,11},{12,13},{... | collective-permute-start | bytes 786440 | tf_op jit(solution)/shard_map/ppermute | solution.py:12
  25.2 1.7 %collective-permute-done.2 = bf16[256,512]{1,0:T(8,128)(2,1)S(1)} collective-permute-done((bf16[256,512]{1,0:T(8,128)(2,1)S(1)}, bf16[256,512]{1,0:T(8,128)(2,1)S(1)}, u32[]{:S(2)}, u32[]{:S(2)}) %collective-permute-start.2) | collective-permute-done | bytes 262176 | tf_op jit(solution)/shard_map/ppermute | solution.py:12
  26.9 1.6 %collective-permute-done.3 = bf16[256,512]{1,0:T(8,128)(2,1)S(1)} collective-permute-done((bf16[256,512]{1,0:T(8,128)(2,1)S(1)}, bf16[256,512]{1,0:T(8,128)(2,1)S(1)}, u32[]{:S(2)}, u32[]{:S(2)}) %collective-permute-start.3) | collective-permute-done | bytes 262176 | tf_op jit(solution)/shard_map/ppermute | solution.py:12
  28.5 0.0 copy-done.2
  28.5 1.3 %fusion.49 = bf16[256,1024]{1,0:T(8,128)(2,1)S(1)} fusion(bf16[2048,2048]{1,0:T(8,128)(2,1)S(1)} %bitcast.13, bf16[256,1024]{1,0:T(8,128)(2,1)S(1)} %slice.92, bf16[256,512]{1,0:T(8,128)(2,1)S(1)} %collective-permute-done.3, bf16[256,512]{1,0:T(8,128)(2,1)S(1)} %collective-permute-done.2, f32[256,2048]{1,0:T(8,128)S(1)} %bitcast.20), kind=kOutput, calls=%fused_computation.32 | convolution fusion | flops 1077411840 | bytes 6815744 | tf_op jit(solution)/shard_map/dot_general | solution.py:16
  29.8 3.1 %collective-permute-start.4 = (bf16[256,512]{1,0:T(8,128)(2,1)S(1)}, bf16[256,512]{1,0:T(8,128)(2,1)S(1)}, u32[]{:S(2)}, u32[]{:S(2)}) collective-permute-start(bf16[256,512]{1,0:T(8,128)(2,1)S(1)} %get-tuple-element.13), channel_id=1, source_target_pairs={{0,4},{4,8},{8,12},{12,16},{16,20},{20,24},{24,28},{1,5},{5,9},{9,... | collective-permute-start | bytes 786440 | tf_op jit(solution)/shard_map/ppermute | solution.py:12
  33.0 4.7 %collective-permute-start.5 = (bf16[256,512]{1,0:T(8,128)(2,1)S(1)}, bf16[256,512]{1,0:T(8,128)(2,1)S(1)}, u32[]{:S(2)}, u32[]{:S(2)}) collective-permute-start(bf16[256,512]{1,0:T(8,128)(2,1)S(1)} %get-tuple-element.14), channel_id=1, source_target_pairs={{0,1},{1,2},{2,3},{4,5},{5,6},{6,7},{8,9},{9,10},{10,11},{12,13},{... | collective-permute-start | bytes 786440 | tf_op jit(solution)/shard_map/ppermute | solution.py:12
  37.6 2.5 %collective-permute-done.4 = bf16[256,512]{1,0:T(8,128)(2,1)S(1)} collective-permute-done((bf16[256,512]{1,0:T(8,128)(2,1)S(1)}, bf16[256,512]{1,0:T(8,128)(2,1)S(1)}, u32[]{:S(2)}, u32[]{:S(2)}) %collective-permute-start.4) | collective-permute-done | bytes 262176 | tf_op jit(solution)/shard_map/ppermute | solution.py:12
  40.1 0.8 collective-permute-done.5
  40.9 1.3 %fusion.46 = bf16[256,1024]{1,0:T(8,128)(2,1)S(1)} fusion(bf16[2048,2048]{1,0:T(8,128)(2,1)S(1)} %bitcast.14, bf16[256,1024]{1,0:T(8,128)(2,1)S(1)} %slice.92, bf16[256,512]{1,0:T(8,128)(2,1)S(1)} %collective-permute-done.5, bf16[256,512]{1,0:T(8,128)(2,1)S(1)} %collective-permute-done.4, f32[256,2048]{1,0:T(8,128)S(1)} %bitcast.21), kind=kOutput, calls=%fused_computation.31 | convolution fusion | flops 1077411840 | bytes 6815744 | tf_op jit(solution)/shard_map/dot_general | solution.py:16
  42.2 2.2 %collective-permute-start.6 = (bf16[256,512]{1,0:T(8,128)(2,1)S(1)}, bf16[256,512]{1,0:T(8,128)(2,1)S(1)}, u32[]{:S(2)}, u32[]{:S(2)}) collective-permute-start(bf16[256,512]{1,0:T(8,128)(2,1)S(1)} %get-tuple-element.11), channel_id=1, source_target_pairs={{0,4},{4,8},{8,12},{12,16},{16,20},{20,24},{24,28},{1,5},{5,9},{9,... | collective-permute-start | bytes 786440 | tf_op jit(solution)/shard_map/ppermute | solution.py:12
  44.5 4.4 %collective-permute-start.7 = (bf16[256,512]{1,0:T(8,128)(2,1)S(1)}, bf16[256,512]{1,0:T(8,128)(2,1)S(1)}, u32[]{:S(2)}, u32[]{:S(2)}) collective-permute-start(bf16[256,512]{1,0:T(8,128)(2,1)S(1)} %get-tuple-element.12), channel_id=1, source_target_pairs={{0,1},{1,2},{2,3},{4,5},{5,6},{6,7},{8,9},{9,10},{10,11},{12,13},{... | collective-permute-start | bytes 786440 | tf_op jit(solution)/shard_map/ppermute | solution.py:12
  48.9 3.6 %collective-permute-done.6 = bf16[256,512]{1,0:T(8,128)(2,1)S(1)} collective-permute-done((bf16[256,512]{1,0:T(8,128)(2,1)S(1)}, bf16[256,512]{1,0:T(8,128)(2,1)S(1)}, u32[]{:S(2)}, u32[]{:S(2)}) %collective-permute-start.6) | collective-permute-done | bytes 262176 | tf_op jit(solution)/shard_map/ppermute | solution.py:12
  52.5 0.0 collective-permute-done.7
  52.5 1.3 %fusion.43 = bf16[256,1024]{1,0:T(8,128)(2,1)S(1)} fusion(bf16[2048,2048]{1,0:T(8,128)(2,1)S(1)} %bitcast.15, bf16[256,1024]{1,0:T(8,128)(2,1)S(1)} %slice.92, f32[256,2048]{1,0:T(8,128)S(1)} %bitcast.22, bf16[256,512]{1,0:T(8,128)(2,1)S(1)} %collective-permute-done.7, bf16[256,512]{1,0:T(8,128)(2,1)S(1)} %collective-permute-done.6), kind=kOutput, calls=%fused_computation.30 | convolution fusion | flops 1077411840 | bytes 6815744 | tf_op jit(solution)/shard_map/dot_general | solution.py:16
  53.8 3.9 %collective-permute-start.8 = (bf16[256,512]{1,0:T(8,128)(2,1)S(1)}, bf16[256,512]{1,0:T(8,128)(2,1)S(1)}, u32[]{:S(2)}, u32[]{:S(2)}) collective-permute-start(bf16[256,512]{1,0:T(8,128)(2,1)S(1)} %get-tuple-element.9), channel_id=1, source_target_pairs={{4,0},{8,4},{12,8},{16,12},{20,16},{24,20},{28,24},{5,1},{9,5},{13... | collective-permute-start | bytes 786440 | tf_op jit(solution)/shard_map/ppermute | solution.py:12
  57.7 1.9 %collective-permute-start.9 = (bf16[256,512]{1,0:T(8,128)(2,1)S(1)}, bf16[256,512]{1,0:T(8,128)(2,1)S(1)}, u32[]{:S(2)}, u32[]{:S(2)}) collective-permute-start(bf16[256,512]{1,0:T(8,128)(2,1)S(1)} %get-tuple-element.10), channel_id=1, source_target_pairs={{1,0},{2,1},{3,2},{5,4},{6,5},{7,6},{9,8},{10,9},{11,10},{13,12},{... | collective-permute-start | bytes 786440 | tf_op jit(solution)/shard_map/ppermute | solution.py:12
  59.7 3.9 %collective-permute-done.8 = bf16[256,512]{1,0:T(8,128)(2,1)S(1)} collective-permute-done((bf16[256,512]{1,0:T(8,128)(2,1)S(1)}, bf16[256,512]{1,0:T(8,128)(2,1)S(1)}, u32[]{:S(2)}, u32[]{:S(2)}) %collective-permute-start.8) | collective-permute-done | bytes 262176 | tf_op jit(solution)/shard_map/ppermute | solution.py:12
  63.6 2.9 %collective-permute-done.9 = bf16[256,512]{1,0:T(8,128)(2,1)S(1)} collective-permute-done((bf16[256,512]{1,0:T(8,128)(2,1)S(1)}, bf16[256,512]{1,0:T(8,128)(2,1)S(1)}, u32[]{:S(2)}, u32[]{:S(2)}) %collective-permute-start.9) | collective-permute-done | bytes 262176 | tf_op jit(solution)/shard_map/ppermute | solution.py:12
  66.4 1.2 %fusion.40 = bf16[256,1024]{1,0:T(8,128)(2,1)S(1)} fusion(bf16[2048,2048]{1,0:T(8,128)(2,1)S(1)} %bitcast.16, bf16[256,512]{1,0:T(8,128)(2,1)S(1)} %collective-permute-done.9, bf16[256,512]{1,0:T(8,128)(2,1)S(1)} %collective-permute-done.8, f32[256,2048]{1,0:T(8,128)S(1)} %bitcast.23, bf16[256,512]{1,0:T(8,128)(2,1)S(1)} %collective-permute-done.7, ...), kind=kOutput, calls=%fused_computation.29 | convolution fusion | flops 1078460416 | bytes 6815744 | tf_op jit(solution)/shard_map/dot_general | solution.py:16
  67.7 2.2 %collective-permute-start.10 = (bf16[256,512]{1,0:T(8,128)(2,1)S(1)}, bf16[256,512]{1,0:T(8,128)(2,1)S(1)}, u32[]{:S(2)}, u32[]{:S(2)}) collective-permute-start(bf16[256,512]{1,0:T(8,128)(2,1)S(1)} %get-tuple-element.7), channel_id=1, source_target_pairs={{4,0},{8,4},{12,8},{16,12},{20,16},{24,20},{28,24},{5,1},{9,5},{13... | collective-permute-start | bytes 786440 | tf_op jit(solution)/shard_map/ppermute | solution.py:12
  69.9 2.3 %collective-permute-start.11 = (bf16[256,512]{1,0:T(8,128)(2,1)S(1)}, bf16[256,512]{1,0:T(8,128)(2,1)S(1)}, u32[]{:S(2)}, u32[]{:S(2)}) collective-permute-start(bf16[256,512]{1,0:T(8,128)(2,1)S(1)} %get-tuple-element.8), channel_id=1, source_target_pairs={{1,0},{2,1},{3,2},{5,4},{6,5},{7,6},{9,8},{10,9},{11,10},{13,12},{... | collective-permute-start | bytes 786440 | tf_op jit(solution)/shard_map/ppermute | solution.py:12
  72.2 3.9 %collective-permute-done.10 = bf16[256,512]{1,0:T(8,128)(2,1)S(1)} collective-permute-done((bf16[256,512]{1,0:T(8,128)(2,1)S(1)}, bf16[256,512]{1,0:T(8,128)(2,1)S(1)}, u32[]{:S(2)}, u32[]{:S(2)}) %collective-permute-start.10) | collective-permute-done | bytes 262176 | tf_op jit(solution)/shard_map/ppermute | solution.py:12
  76.1 1.5 %collective-permute-done.11 = bf16[256,512]{1,0:T(8,128)(2,1)S(1)} collective-permute-done((bf16[256,512]{1,0:T(8,128)(2,1)S(1)}, bf16[256,512]{1,0:T(8,128)(2,1)S(1)}, u32[]{:S(2)}, u32[]{:S(2)}) %collective-permute-start.11) | collective-permute-done | bytes 262176 | tf_op jit(solution)/shard_map/ppermute | solution.py:12
  77.6 1.2 %fusion.37 = bf16[256,1024]{1,0:T(8,128)(2,1)S(1)} fusion(bf16[2048,2048]{1,0:T(8,128)(2,1)S(1)} %bitcast.17, bf16[256,512]{1,0:T(8,128)(2,1)S(1)} %collective-permute-done.11, bf16[256,512]{1,0:T(8,128)(2,1)S(1)} %collective-permute-done.10, f32[256,2048]{1,0:T(8,128)S(1)} %bitcast.24, bf16[256,512]{1,0:T(8,128)(2,1)S(1)} %collective-permute-done.7, ...), kind=kOutput, calls=%fused_computation.28 | convolution fusion | flops 1078460416 | bytes 6815744 | tf_op jit(solution)/shard_map/dot_general | solution.py:16
  78.9 3.3 %collective-permute-start.12 = (bf16[256,512]{1,0:T(8,128)(2,1)S(1)}, bf16[256,512]{1,0:T(8,128)(2,1)S(1)}, u32[]{:S(2)}, u32[]{:S(2)}) collective-permute-start(bf16[256,512]{1,0:T(8,128)(2,1)S(1)} %get-tuple-element.5), channel_id=1, source_target_pairs={{4,0},{8,4},{12,8},{16,12},{20,16},{24,20},{28,24},{5,1},{9,5},{13... | collective-permute-start | bytes 786440 | tf_op jit(solution)/shard_map/ppermute | solution.py:12
  82.2 2.7 %collective-permute-start.13 = (bf16[256,512]{1,0:T(8,128)(2,1)S(1)}, bf16[256,512]{1,0:T(8,128)(2,1)S(1)}, u32[]{:S(2)}, u32[]{:S(2)}) collective-permute-start(bf16[256,512]{1,0:T(8,128)(2,1)S(1)} %get-tuple-element.6), channel_id=1, source_target_pairs={{1,0},{2,1},{3,2},{5,4},{6,5},{7,6},{9,8},{10,9},{11,10},{13,12},{... | collective-permute-start | bytes 786440 | tf_op jit(solution)/shard_map/ppermute | solution.py:12
  84.9 3.2 %collective-permute-done.12 = bf16[256,512]{1,0:T(8,128)(2,1)S(1)} collective-permute-done((bf16[256,512]{1,0:T(8,128)(2,1)S(1)}, bf16[256,512]{1,0:T(8,128)(2,1)S(1)}, u32[]{:S(2)}, u32[]{:S(2)}) %collective-permute-start.12) | collective-permute-done | bytes 262176 | tf_op jit(solution)/shard_map/ppermute | solution.py:12
  88.1 1.8 %collective-permute-done.13 = bf16[256,512]{1,0:T(8,128)(2,1)S(1)} collective-permute-done((bf16[256,512]{1,0:T(8,128)(2,1)S(1)}, bf16[256,512]{1,0:T(8,128)(2,1)S(1)}, u32[]{:S(2)}, u32[]{:S(2)}) %collective-permute-start.13) | collective-permute-done | bytes 262176 | tf_op jit(solution)/shard_map/ppermute | solution.py:12
  89.9 3.3 %fusion.15 = bf16[1,1,256,2048]{3,2,1,0:T(8,128)(2,1)} fusion(bf16[256,512]{1,0:T(8,128)(2,1)S(1)} %collective-permute-done.13, bf16[256,512]{1,0:T(8,128)(2,1)S(1)} %collective-permute-done.12, bf16[256,512]{1,0:T(8,128)(2,1)S(1)} %collective-permute-done.7, bf16[256,512]{1,0:T(8,128)(2,1)S(1)} %collective-permute-done.6, ...), kind=kOutput, calls=%fused_computation.16 | convolution fusion | flops 2152726528 | bytes 12582912 | tf_op jit(solution)/shard_map/dot_general | solution.py:16
  (8 shorter events, 0.3 us)
Async XLA Ops:
  0.0 11.5 %copy-start = (bf16[1,1,256,2048]{3,2,1,0:T(8,128)(2,1)S(1)}, bf16[1,1,256,2048]{3,2,1,0:T(8,128)(2,1)}, u32[]{:S(2)}) copy-start(bf16[1,1,256,2048]{3,2,1,0:T(8,128)(2,1)} %param.5) | copy-start | bytes 3145732
  0.0 14.8 %copy-start.1 = (bf16[1,1,2048,2048]{3,2,1,0:T(8,128)(2,1)S(1)}, bf16[1,1,2048,2048]{3,2,1,0:T(8,128)(2,1)}, u32[]{:S(2)}) copy-start(bf16[1,1,2048,2048]{3,2,1,0:T(8,128)(2,1)} %param.3) | copy-start | bytes 25165828
  4.3 10.1 %collective-permute-start = (bf16[256,512]{1,0:T(8,128)(2,1)S(1)}, bf16[256,512]{1,0:T(8,128)(2,1)S(1)}, u32[]{:S(2)}, u32[]{:S(2)}) collective-permute-start(bf16[256,512]{1,0:T(8,128)(2,1)S(1)} %get-tuple-element.17), channel_id=1, source_target_pairs={{0,4},{4,8},{8,12},{12,16},{16,20},{20,24},{24,28},{1,5},{5,9},{9,... | collective-permute-start | bytes 786440 | tf_op jit(solution)/shard_map/ppermute | solution.py:12
  7.5 7.3 %collective-permute-start.1 = (bf16[256,512]{1,0:T(8,128)(2,1)S(1)}, bf16[256,512]{1,0:T(8,128)(2,1)S(1)}, u32[]{:S(2)}, u32[]{:S(2)}) collective-permute-start(bf16[256,512]{1,0:T(8,128)(2,1)S(1)} %get-tuple-element.18), channel_id=1, source_target_pairs={{0,1},{1,2},{2,3},{4,5},{5,6},{6,7},{8,9},{9,10},{10,11},{12,13},{... | collective-permute-start | bytes 786440 | tf_op jit(solution)/shard_map/ppermute | solution.py:12
  11.6 17.0 %copy-start.2 = (f32[1,1,256,2048]{3,2,1,0:T(8,128)S(1)}, f32[1,1,256,2048]{3,2,1,0:T(8,128)}, u32[]{:S(2)}) copy-start(f32[1,1,256,2048]{3,2,1,0:T(8,128)} %param.4) | copy-start | bytes 6291460
  17.4 9.6 %collective-permute-start.2 = (bf16[256,512]{1,0:T(8,128)(2,1)S(1)}, bf16[256,512]{1,0:T(8,128)(2,1)S(1)}, u32[]{:S(2)}, u32[]{:S(2)}) collective-permute-start(bf16[256,512]{1,0:T(8,128)(2,1)S(1)} %get-tuple-element.15), channel_id=1, source_target_pairs={{0,4},{4,8},{8,12},{12,16},{16,20},{20,24},{24,28},{1,5},{5,9},{9,... | collective-permute-start | bytes 786440 | tf_op jit(solution)/shard_map/ppermute | solution.py:12
  20.5 8.0 %collective-permute-start.3 = (bf16[256,512]{1,0:T(8,128)(2,1)S(1)}, bf16[256,512]{1,0:T(8,128)(2,1)S(1)}, u32[]{:S(2)}, u32[]{:S(2)}) collective-permute-start(bf16[256,512]{1,0:T(8,128)(2,1)S(1)} %get-tuple-element.16), channel_id=1, source_target_pairs={{0,1},{1,2},{2,3},{4,5},{5,6},{6,7},{8,9},{9,10},{10,11},{12,13},{... | collective-permute-start | bytes 786440 | tf_op jit(solution)/shard_map/ppermute | solution.py:12
  29.8 10.3 %collective-permute-start.4 = (bf16[256,512]{1,0:T(8,128)(2,1)S(1)}, bf16[256,512]{1,0:T(8,128)(2,1)S(1)}, u32[]{:S(2)}, u32[]{:S(2)}) collective-permute-start(bf16[256,512]{1,0:T(8,128)(2,1)S(1)} %get-tuple-element.13), channel_id=1, source_target_pairs={{0,4},{4,8},{8,12},{12,16},{16,20},{20,24},{24,28},{1,5},{5,9},{9,... | collective-permute-start | bytes 786440 | tf_op jit(solution)/shard_map/ppermute | solution.py:12
  33.0 8.0 %collective-permute-start.5 = (bf16[256,512]{1,0:T(8,128)(2,1)S(1)}, bf16[256,512]{1,0:T(8,128)(2,1)S(1)}, u32[]{:S(2)}, u32[]{:S(2)}) collective-permute-start(bf16[256,512]{1,0:T(8,128)(2,1)S(1)} %get-tuple-element.14), channel_id=1, source_target_pairs={{0,1},{1,2},{2,3},{4,5},{5,6},{6,7},{8,9},{9,10},{10,11},{12,13},{... | collective-permute-start | bytes 786440 | tf_op jit(solution)/shard_map/ppermute | solution.py:12
  42.2 10.2 %collective-permute-start.6 = (bf16[256,512]{1,0:T(8,128)(2,1)S(1)}, bf16[256,512]{1,0:T(8,128)(2,1)S(1)}, u32[]{:S(2)}, u32[]{:S(2)}) collective-permute-start(bf16[256,512]{1,0:T(8,128)(2,1)S(1)} %get-tuple-element.11), channel_id=1, source_target_pairs={{0,4},{4,8},{8,12},{12,16},{16,20},{20,24},{24,28},{1,5},{5,9},{9,... | collective-permute-start | bytes 786440 | tf_op jit(solution)/shard_map/ppermute | solution.py:12
  44.5 8.0 %collective-permute-start.7 = (bf16[256,512]{1,0:T(8,128)(2,1)S(1)}, bf16[256,512]{1,0:T(8,128)(2,1)S(1)}, u32[]{:S(2)}, u32[]{:S(2)}) collective-permute-start(bf16[256,512]{1,0:T(8,128)(2,1)S(1)} %get-tuple-element.12), channel_id=1, source_target_pairs={{0,1},{1,2},{2,3},{4,5},{5,6},{6,7},{8,9},{9,10},{10,11},{12,13},{... | collective-permute-start | bytes 786440 | tf_op jit(solution)/shard_map/ppermute | solution.py:12
  53.8 9.8 %collective-permute-start.8 = (bf16[256,512]{1,0:T(8,128)(2,1)S(1)}, bf16[256,512]{1,0:T(8,128)(2,1)S(1)}, u32[]{:S(2)}, u32[]{:S(2)}) collective-permute-start(bf16[256,512]{1,0:T(8,128)(2,1)S(1)} %get-tuple-element.9), channel_id=1, source_target_pairs={{4,0},{8,4},{12,8},{16,12},{20,16},{24,20},{28,24},{5,1},{9,5},{13... | collective-permute-start | bytes 786440 | tf_op jit(solution)/shard_map/ppermute | solution.py:12
  57.7 8.7 %collective-permute-start.9 = (bf16[256,512]{1,0:T(8,128)(2,1)S(1)}, bf16[256,512]{1,0:T(8,128)(2,1)S(1)}, u32[]{:S(2)}, u32[]{:S(2)}) collective-permute-start(bf16[256,512]{1,0:T(8,128)(2,1)S(1)} %get-tuple-element.10), channel_id=1, source_target_pairs={{1,0},{2,1},{3,2},{5,4},{6,5},{7,6},{9,8},{10,9},{11,10},{13,12},{... | collective-permute-start | bytes 786440 | tf_op jit(solution)/shard_map/ppermute | solution.py:12
  67.7 8.4 %collective-permute-start.10 = (bf16[256,512]{1,0:T(8,128)(2,1)S(1)}, bf16[256,512]{1,0:T(8,128)(2,1)S(1)}, u32[]{:S(2)}, u32[]{:S(2)}) collective-permute-start(bf16[256,512]{1,0:T(8,128)(2,1)S(1)} %get-tuple-element.7), channel_id=1, source_target_pairs={{4,0},{8,4},{12,8},{16,12},{20,16},{24,20},{28,24},{5,1},{9,5},{13... | collective-permute-start | bytes 786440 | tf_op jit(solution)/shard_map/ppermute | solution.py:12
  69.9 7.7 %collective-permute-start.11 = (bf16[256,512]{1,0:T(8,128)(2,1)S(1)}, bf16[256,512]{1,0:T(8,128)(2,1)S(1)}, u32[]{:S(2)}, u32[]{:S(2)}) collective-permute-start(bf16[256,512]{1,0:T(8,128)(2,1)S(1)} %get-tuple-element.8), channel_id=1, source_target_pairs={{1,0},{2,1},{3,2},{5,4},{6,5},{7,6},{9,8},{10,9},{11,10},{13,12},{... | collective-permute-start | bytes 786440 | tf_op jit(solution)/shard_map/ppermute | solution.py:12
  78.9 9.2 %collective-permute-start.12 = (bf16[256,512]{1,0:T(8,128)(2,1)S(1)}, bf16[256,512]{1,0:T(8,128)(2,1)S(1)}, u32[]{:S(2)}, u32[]{:S(2)}) collective-permute-start(bf16[256,512]{1,0:T(8,128)(2,1)S(1)} %get-tuple-element.5), channel_id=1, source_target_pairs={{4,0},{8,4},{12,8},{16,12},{20,16},{24,20},{28,24},{5,1},{9,5},{13... | collective-permute-start | bytes 786440 | tf_op jit(solution)/shard_map/ppermute | solution.py:12
  82.2 7.7 %collective-permute-start.13 = (bf16[256,512]{1,0:T(8,128)(2,1)S(1)}, bf16[256,512]{1,0:T(8,128)(2,1)S(1)}, u32[]{:S(2)}, u32[]{:S(2)}) collective-permute-start(bf16[256,512]{1,0:T(8,128)(2,1)S(1)} %get-tuple-element.6), channel_id=1, source_target_pairs={{1,0},{2,1},{3,2},{5,4},{6,5},{7,6},{9,8},{10,9},{11,10},{13,12},{... | collective-permute-start | bytes 786440 | tf_op jit(solution)/shard_map/ppermute | solution.py:12
where the time goes:
time: 93.8 us; the launch traced here: 93.2 us
  starting transfers between devices  45.8 us (49%)
  waiting for transfers between devices  30.5 us (33%)
  matrix products  16.3 us (17%)
    ppermute x14, starting transfers between devices, from_behind(): return lax.ppermute(array, axis, pairs)  45.8 us
    ppermute x14, waiting for transfers between devices, from_behind(): return lax.ppermute(array, axis, pairs)  30.5 us
    dot_general x8, matrix products, project(): jnp.dot(state, weights[:, low:low + width], preferred_element_type=jnp.fl...  16.3 us
  transfers between devices with their start and end apart: 14, of which 13 were waited for; matrix products, arithmetic and copies ran while one was open for 0% of the time, Pallas kernels for 0%

commit v1 on v0

v1 whole, which is shorter than its diff:
```python
import functools

import jax
import jax.numpy as jnp
from jax import lax
from jax.experimental import pallas as pl
from jax.experimental.pallas import tpu as pltpu
from jax.sharding import PartitionSpec as P

TICKS = 8
CHUNKS = 4
MESH = pl.DeviceIdType.MESH


def dot(a, b):
    return jnp.dot(a, b, preferred_element_type=jnp.float32)


def sweep(
    maps_hbm, sources_hbm, traces_hbm, out_hbm,
    maps, sources, traces, held_down, held_up, held_last, first_up, result,
    send_x, send_y, recv_x, recv_y,
    maps_sem, sources_sem, traces_sem, out_sem, ssx, ssy, rsx, rsy,
):
    face = traces.shape[-1] // 4
    rows = traces.shape[1]
    last = TICKS - 1
    turn = TICKS // 2
    low, high = slice(0, 2 * face), slice(2 * face, 4 * face)
    i, j = lax.axis_index("gx"), lax.axis_index("gy")
    px, py = lax.axis_size("gx"), lax.axis_size("gy")
    has_left, has_right = i > 0, i < px - 1
    has_below, has_above = j > 0, j < py - 1

    def load_maps(row, col, col_faces, sem):
        window = (pl.ds(row * face, 2 * face), pl.ds(col * face, col_faces * face))
        return pltpu.make_async_copy(maps_hbm.at[(0, 0) + window], maps.at[window], maps_sem.at[sem])

    def load_sources(col, col_faces, sem):
        columns = pl.ds(col * face, col_faces * face)
        return [
            pltpu.make_async_copy(
                sources_hbm.at[0, 0, pl.ds(c * rows, rows), columns], sources.at[c, :, columns], sources_sem.at[sem, c]
            )
            for c in range(CHUNKS)
        ]

    load_traces = [
        pltpu.make_async_copy(traces_hbm.at[0, 0, pl.ds(c * rows, rows)], traces.at[c], traces_sem.at[c])
        for c in range(CHUNKS)
    ]
    east_sources, north_sources, low_sources = load_sources(2, 1, 0), load_sources(3, 1, 1), load_sources(0, 2, 2)
    high_east, low_east = load_maps(2, 2, 1, 0), load_maps(0, 2, 1, 1)
    high_north, low_north = load_maps(2, 3, 1, 2), load_maps(0, 3, 1, 3)
    high_low, low_low = load_maps(2, 0, 2, 4), load_maps(0, 0, 2, 5)
    for copy in load_traces + [high_east] + east_sources + [low_east, high_north] + north_sources + [low_north]:
        copy.start()
    for copy in [high_low] + low_sources + [low_low]:
        copy.start()

    barrier = pltpu.get_barrier_semaphore()
    neighbours = ((has_left, "gx", i - 1), (has_right, "gx", i + 1), (has_below, "gy", j - 1), (has_above, "gy", j + 1))
    for there, axis, index in neighbours:
        @pl.when(there)
        def _():
            pl.semaphore_signal(barrier, inc=1, device_id={axis: index}, device_id_type=MESH)
    pl.semaphore_wait(barrier, sum(there.astype(jnp.int32) for there, _, _ in neighbours))

    def copy_x(t, c, target):
        return pltpu.make_async_remote_copy(
            src_ref=send_x.at[t, c], dst_ref=recv_x.at[t, c], send_sem=ssx.at[t, c], recv_sem=rsx.at[t, c],
            device_id={"gx": target}, device_id_type=MESH,
        )

    def copy_y(t, c, target):
        return pltpu.make_async_remote_copy(
            src_ref=send_y.at[t, c], dst_ref=recv_y.at[t, c], send_sem=ssy.at[t, c], recv_sem=rsy.at[t, c],
            device_id={"gy": target}, device_id_type=MESH,
        )

    def put(copy, there, buffer, t, c, value, target):
        buffer[t, c] = value.astype(buffer.dtype)

        @pl.when(there)
        def _():
            copy(t, c, target).start()

    put_east = functools.partial(put, copy_x, has_right, send_x, target=i + 1)
    put_north = functools.partial(put, copy_y, has_above, send_y, target=j + 1)
    put_west = functools.partial(put, copy_x, has_left, send_x, target=i - 1)
    put_south = functools.partial(put, copy_y, has_below, send_y, target=j - 1)

    def await_faces(t, c, there_x, there_y):
        @pl.when(there_y)
        def _():
            copy_y(t, c, j).wait_recv()

        @pl.when(there_x)
        def _():
            copy_x(t, c, i).wait_recv()

    def clear(buffer, there, begin, end):
        @pl.when(jnp.logical_not(there))
        def _():
            buffer[begin:end] = jnp.zeros((end - begin,) + buffer.shape[1:], buffer.dtype)

    def cols(k):
        return slice(k * face, (k + 1) * face)

    for k, put_face, high_copy, low_copy, source_copies in (
        (2, put_east, high_east, low_east, east_sources),
        (3, put_north, high_north, low_north, north_sources),
    ):
        if k == 2:
            for copy in load_traces:
                copy.wait()
        high_copy.wait()
        low_copy.wait()
        for copy in source_copies:
            copy.wait()

        def first(c, carry):
            held_down[c, :, cols(k - 2)] = dot(traces[c, :, high], maps[high, cols(k)]) + sources[c, :, cols(k)]
            put_face(0, c, dot(traces[c, :, low], maps[low, cols(k)]) + held_down[c, :, cols(k - 2)])
            return carry

        lax.fori_loop(0, CHUNKS, first, 0)

    clear(recv_x, has_left, 0, turn)
    clear(recv_y, has_below, 0, turn)
    clear(recv_x, has_right, turn, last)
    clear(recv_y, has_above, turn, last)

    high_low.wait()
    low_low.wait()
    for copy in low_sources:
        copy.wait()

    def ahead(c, carry):
        first_up[c] = dot(traces[c, :, high], maps[high, low]) + sources[c, :, low]
        return carry

    def arrived(t, c, row, columns):
        x = dot(recv_x[t, c], maps[row * face : (row + 1) * face, columns])
        y = dot(recv_y[t, c], maps[(row + 1) * face : (row + 2) * face, columns])
        return x + y

    def down(step, carry):
        t, c = step // CHUNKS + 1, step % CHUNKS
        await_faces(t - 1, c, has_left, has_below)
        put_east(t, c, arrived(t - 1, c, 0, cols(2)) + held_down[c, :, cols(0)])
        put_north(t, c, arrived(t - 1, c, 0, cols(3)) + held_down[c, :, cols(1)])
        return carry

    lax.fori_loop(0, CHUNKS, down, 0)
    lax.fori_loop(0, CHUNKS, ahead, 0)
    lax.fori_loop(CHUNKS, (turn - 1) * CHUNKS, down, 0)

    def turned(c, carry):
        await_faces(turn - 1, c, has_left, has_below)
        for k, put_face in ((0, put_west), (1, put_south)):
            value = arrived(turn - 1, c, 0, cols(k))
            put_face(turn, c, value + first_up[c, :, cols(k)])
            held_up[c, :, cols(k)] = value + sources[c, :, cols(k)]
        return carry

    lax.fori_loop(0, CHUNKS, turned, 0)

    def late(c, carry):
        held_last[c] = arrived(turn - 1, c, 0, high) + sources[c, :, high]
        return carry

    def up(step, carry):
        t, c = step // CHUNKS + turn + 1, step % CHUNKS
        await_faces(t - 1, c, has_right, has_above)
        put_west(t, c, arrived(t - 1, c, 2, cols(0)) + held_up[c, :, cols(0)])
        put_south(t, c, arrived(t - 1, c, 2, cols(1)) + held_up[c, :, cols(1)])
        return carry

    lax.fori_loop(0, CHUNKS, up, 0)
    lax.fori_loop(0, CHUNKS, late, 0)
    lax.fori_loop(CHUNKS, (last - turn - 1) * CHUNKS, up, 0)

    def store_out(c):
        return pltpu.make_async_copy(result.at[c], out_hbm.at[0, 0, pl.ds(c * rows, rows)], out_sem.at[c])

    for c in range(CHUNKS):
        await_faces(last - 1, c, has_right, has_above)
        result[c, :, low] = (arrived(last - 1, c, 2, low) + held_up[c]).astype(result.dtype)
        result[c, :, high] = (arrived(last - 1, c, 2, high) + held_last[c]).astype(result.dtype)
        store_out(c).start()

    def sent(begin, end, there_x, there_y):
        def one(step, carry):
            t, c = step // CHUNKS + begin, step % CHUNKS

            @pl.when(there_x)
            def _():
                copy_x(t, c, i).wait_send()

            @pl.when(there_y)
            def _():
                copy_y(t, c, j).wait_send()

            return carry

        lax.fori_loop(0, (end - begin) * CHUNKS, one, 0)

    sent(0, turn, has_right, has_above)
    sent(turn, last, has_left, has_below)
    for c in range(CHUNKS):
        store_out(c).wait()


def on_device(maps, sources, traces):
    total, width = traces.shape[2:]
    face = width // 4
    rows = total // CHUNKS
    swaps = TICKS - 1

    def faces():
        return pltpu.VMEM((swaps, CHUNKS, rows, face), jnp.bfloat16)

    def wide(columns, dtype):
        return pltpu.VMEM((CHUNKS, rows, columns), dtype)

    dma = pltpu.SemaphoreType.DMA
    return pl.pallas_call(
        sweep,
        out_shape=jax.ShapeDtypeStruct(traces.shape, jnp.bfloat16),
        in_specs=[pl.BlockSpec(memory_space=pl.ANY)] * 3,
        out_specs=pl.BlockSpec(memory_space=pl.ANY),
        scratch_shapes=[
            pltpu.VMEM((width, width), jnp.bfloat16),
            wide(width, jnp.float32),
            wide(width, jnp.bfloat16),
            wide(2 * face, jnp.float32),
            wide(2 * face, jnp.float32),
            wide(2 * face, jnp.float32),
            wide(2 * face, jnp.float32),
            wide(width, jnp.bfloat16),
            faces(),
            faces(),
            faces(),
            faces(),
            dma((6,)),
            dma((3, CHUNKS)),
            dma((CHUNKS,)),
            dma((CHUNKS,)),
        ]
        + [dma((swaps, CHUNKS))] * 4,
        compiler_params=pltpu.CompilerParams(collective_id=0, has_side_effects=True),
    )(maps, sources, traces)


def solution(mesh):
    spec = P("gx", "gy", None, None)
    return jax.shard_map(on_device, mesh=mesh, in_specs=(spec, spec, spec), out_specs=spec, check_vma=False)
```

time: 93.8 us -> 58.8 us (0.63)
  Pallas kernels: 0 us -> 56.4 us
  starting transfers between devices: 45.8 us -> 0 us
  waiting for transfers between devices: 30.5 us -> 0 us
  matrix products: 16.3 us -> 0 us
  local copies, waits for them, and re-layouts: 0.31 us -> 2.3 us
    pallas_call x0 -> x1, Pallas kernels: none -> 56.4 us  [on_device(): pl.pallas_call(sweep, out_shape=jax.ShapeDtypeStruct(traces.shape, jnp.bf...]
    ppermute x14 -> x0, starting transfers between devices: 45.8 us -> none  [from_behind(): return lax.ppermute(array, axis, pairs)]
    ppermute x14 -> x0, waiting for transfers between devices: 30.5 us -> none  [from_behind(): return lax.ppermute(array, axis, pairs)]
    dot_general x8 -> x0, matrix products: 16.3 us -> none  [project(): jnp.dot(state, weights[:, low:low + width], preferred_element_type=jnp.fl...]
    unnamed x6 -> x1, local copies, waits for them, and re-layouts: 0.01 us -> 2.3 us
  transfers between devices with their start and end apart: 14 -> 0, of which waited for: 13 -> 0; matrix products, arithmetic and copies ran while one was open for 0% -> 0% of each run, Pallas kernels for 0% -> 0%
where the time goes in v1:
time: 58.8 us; the launch traced here: 58.7 us
  Pallas kernels  56.4 us (96%)
  local copies, waits for them, and re-layouts  2.3 us (4%)
    pallas_call x1, Pallas kernels, on_device(): pl.pallas_call(sweep, out_shape=jax.ShapeDtypeStruct(traces.shape, jnp.bf...  56.4 us
    unnamed x1, local copies, waits for them, and re-layouts  2.3 us

profile of v1, /device:TPU:17, one launch (start us, length us, event | category | flops | bytes accessed | tf_op | source)
XLA Modules:
  0.0 58.7 jit_solution(8785892130500877939)
XLA Ops:
  0.0 56.4 %shard_map.37 = bf16[1,1,256,2048]{3,2,1,0:T(8,128)(2,1)} custom-call(bf16[1,1,2048,2048]{3,2,1,0:T(8,128)(2,1)} %maps_hbm.1, f32[1,1,256,2048]{3,2,1,0:T(8,128)} %sources_hbm.1, bf16[1,1,256,2048]{3,2,1,0:T(8,128)(2,1)} %traces_hbm.1), custom_call_target="tpu_custom_call" | custom-call | tf_op jit(solution)/shard_map/pallas_call | solution.py:228
  56.4 2.3 %copy.5 = bf16[1,1,256,2048]{3,2,1,0:T(8,128)(2,1)} copy(bf16[1,1,256,2048]{3,2,1,0:T(8,128)(2,1)} %shard_map.37) | data formatting | bytes 2097152

commit v2 on v1

--- a/solution.py
+++ b/solution.py
@@ -8,7 +8,7 @@
 from jax.sharding import PartitionSpec as P
 
 TICKS = 8
-CHUNKS = 4
+CHUNKS = 2
 MESH = pl.DeviceIdType.MESH
 
 
@@ -18,7 +18,7 @@
 
 def sweep(
     maps_hbm, sources_hbm, traces_hbm, out_hbm,
-    maps, sources, traces, held_down, held_up, held_last, first_up, result,
+    maps, sources, traces, held_down, held_up, held_last, first_up, partial, result,
     send_x, send_y, recv_x, recv_y,
     maps_sem, sources_sem, traces_sem, out_sem, ssx, ssy, rsx, rsy,
 ):
@@ -90,12 +90,13 @@
     put_west = functools.partial(put, copy_x, has_left, send_x, target=i - 1)
     put_south = functools.partial(put, copy_y, has_below, send_y, target=j - 1)
 
-    def await_faces(t, c, there_x, there_y):
-        @pl.when(there_y)
+    def await_y(t, c, there):
+        @pl.when(there)
         def _():
             copy_y(t, c, j).wait_recv()
 
-        @pl.when(there_x)
+    def await_x(t, c, there):
+        @pl.when(there)
         def _():
             copy_x(t, c, i).wait_recv()
 
@@ -136,58 +137,68 @@
     for copy in low_sources:
         copy.wait()
 
-    def ahead(c, carry):
+    def from_x(t, c, row, columns):
+        return dot(recv_x[t, c], maps[row * face : (row + 1) * face, columns])
+
+    def from_y(t, c, row, columns):
+        return dot(recv_y[t, c], maps[(row + 1) * face : (row + 2) * face, columns])
+
+    def down(step, carry, extra=None):
+        t, c = step // CHUNKS + 1, step % CHUNKS
+        await_y(t - 1, c, has_below)
+        partial[...] = from_y(t - 1, c, 0, high) + held_down[c]
+        await_x(t - 1, c, has_left)
+        put_east(t, c, from_x(t - 1, c, 0, cols(2)) + partial[:, cols(0)])
+        put_north(t, c, from_x(t - 1, c, 0, cols(3)) + partial[:, cols(1)])
+        if extra is not None:
+            extra(c)
+        return carry
+
+    def ahead(c):
         first_up[c] = dot(traces[c, :, high], maps[high, low]) + sources[c, :, low]
+
+    lax.fori_loop(0, CHUNKS, functools.partial(down, extra=ahead), 0)
+    lax.fori_loop(CHUNKS, (turn - 1) * CHUNKS, down, 0)
+
+    def turned(c, carry):
+        await_y(turn - 1, c, has_below)
+        partial[...] = from_y(turn - 1, c, 0, low)
+        await_x(turn - 1, c, has_left)
+        for k, put_face in ((0, put_west), (1, put_south)):
+            partial[:, cols(k)] += from_x(turn - 1, c, 0, cols(k))
+            put_face(turn, c, partial[:, cols(k)] + first_up[c, :, cols(k)])
+        held_up[c] = partial[...] + sources[c, :, low]
         return carry
 
-    def arrived(t, c, row, columns):
-        x = dot(recv_x[t, c], maps[row * face : (row + 1) * face, columns])
-        y = dot(recv_y[t, c], maps[(row + 1) * face : (row + 2) * face, columns])
-        return x + y
-
-    def down(step, carry):
-        t, c = step // CHUNKS + 1, step % CHUNKS
-        await_faces(t - 1, c, has_left, has_below)
-        put_east(t, c, arrived(t - 1, c, 0, cols(2)) + held_down[c, :, cols(0)])
-        put_north(t, c, arrived(t - 1, c, 0, cols(3)) + held_down[c, :, cols(1)])
+    lax.fori_loop(0, CHUNKS, turned, 0)
+
+    def late(c):
+        held_last[c] = from_x(turn - 1, c, 0, high) + from_y(turn - 1, c, 0, high) + sources[c, :, high]
+
+    def up(step, carry, extra=None):
+        t, c = step // CHUNKS + turn + 1, step % CHUNKS
+        await_y(t - 1, c, has_above)
+        partial[...] = from_y(t - 1, c, 2, low) + held_up[c]
+        await_x(t - 1, c, has_right)
+        put_west(t, c, from_x(t - 1, c, 2, cols(0)) + partial[:, cols(0)])
+        put_south(t, c, from_x(t - 1, c, 2, cols(1)) + partial[:, cols(1)])
+        if extra is not None:
+            extra(c)
         return carry
 
-    lax.fori_loop(0, CHUNKS, down, 0)
-    lax.fori_loop(0, CHUNKS, ahead, 0)
-    lax.fori_loop(CHUNKS, (turn - 1) * CHUNKS, down, 0)
-
-    def turned(c, carry):
-        await_faces(turn - 1, c, has_left, has_below)
-        for k, put_face in ((0, put_west), (1, put_south)):
-            value = arrived(turn - 1, c, 0, cols(k))
-            put_face(turn, c, value + first_up[c, :, cols(k)])
-            held_up[c, :, cols(k)] = value + sources[c, :, cols(k)]
-        return carry
-
-    lax.fori_loop(0, CHUNKS, turned, 0)
-
-    def late(c, carry):
-        held_last[c] = arrived(turn - 1, c, 0, high) + sources[c, :, high]
-        return carry
-
-    def up(step, carry):
-        t, c = step // CHUNKS + turn + 1, step % CHUNKS
-        await_faces(t - 1, c, has_right, has_above)
-        put_west(t, c, arrived(t - 1, c, 2, cols(0)) + held_up[c, :, cols(0)])
-        put_south(t, c, arrived(t - 1, c, 2, cols(1)) + held_up[c, :, cols(1)])
-        return carry
-
-    lax.fori_loop(0, CHUNKS, up, 0)
-    lax.fori_loop(0, CHUNKS, late, 0)
+    lax.fori_loop(0, CHUNKS, functools.partial(up, extra=late), 0)
     lax.fori_loop(CHUNKS, (last - turn - 1) * CHUNKS, up, 0)
 
     def store_out(c):
         return pltpu.make_async_copy(result.at[c], out_hbm.at[0, 0, pl.ds(c * rows, rows)], out_sem.at[c])
 
     for c in range(CHUNKS):
-        await_faces(last - 1, c, has_right, has_above)
-        result[c, :, low] = (arrived(last - 1, c, 2, low) + held_up[c]).astype(result.dtype)
-        result[c, :, high] = (arrived(last - 1, c, 2, high) + held_last[c]).astype(result.dtype)
+        await_y(last - 1, c, has_above)
+        held_up[c] += from_y(last - 1, c, 2, low)
+        held_last[c] += from_y(last - 1, c, 2, high)
+        await_x(last - 1, c, has_right)
+        result[c, :, low] = (from_x(last - 1, c, 2, low) + held_up[c]).astype(result.dtype)
+        result[c, :, high] = (from_x(last - 1, c, 2, high) + held_last[c]).astype(result.dtype)
         store_out(c).start()
 
     def sent(begin, end, there_x, there_y):
@@ -238,6 +249,7 @@
             wide(2 * face, jnp.float32),
             wide(2 * face, jnp.float32),
             wide(2 * face, jnp.float32),
+            pltpu.VMEM((rows, 2 * face), jnp.float32),
             wide(width, jnp.bfloat16),
             faces(),
             faces(),

time: 58.8 us -> 51.7 us (0.88); the launches traced: 58.7 us -> 50.8 us
  Pallas kernels: 56.4 us -> 48.5 us
    pallas_call x1, Pallas kernels: 56.4 us -> 48.5 us  [on_device(): pl.pallas_call(sweep, out_shape=jax.ShapeDtypeStruct(traces.shape, jnp.bf...]
where the time goes in v2:
time: 51.7 us; the launch traced here: 50.8 us
  Pallas kernels  48.5 us (94%)
  local copies, waits for them, and re-layouts  2.3 us (4%)
    pallas_call x1, Pallas kernels, on_device(): pl.pallas_call(sweep, out_shape=jax.ShapeDtypeStruct(traces.shape, jnp.bf...  48.5 us
    unnamed x1, local copies, waits for them, and re-layouts  2.3 us

profile of v2, /device:TPU:17, one launch (start us, length us, event | category | flops | bytes accessed | tf_op | source)
XLA Modules:
  0.0 50.8 jit_solution(16958979308380760951)
XLA Ops:
  0.0 48.5 %shard_map.37 = bf16[1,1,256,2048]{3,2,1,0:T(8,128)(2,1)} custom-call(bf16[1,1,2048,2048]{3,2,1,0:T(8,128)(2,1)} %maps_hbm.1, f32[1,1,256,2048]{3,2,1,0:T(8,128)} %sources_hbm.1, bf16[1,1,256,2048]{3,2,1,0:T(8,128)(2,1)} %traces_hbm.1), custom_call_target="tpu_custom_call" | custom-call | tf_op jit(solution)/shard_map/pallas_call | solution.py:239
  48.5 2.3 %copy.5 = bf16[1,1,256,2048]{3,2,1,0:T(8,128)(2,1)} copy(bf16[1,1,256,2048]{3,2,1,0:T(8,128)(2,1)} %shard_map.37) | data formatting | bytes 2097152

commit v3 on v2

--- a/solution.py
+++ b/solution.py
@@ -53,9 +53,7 @@
     high_east, low_east = load_maps(2, 2, 1, 0), load_maps(0, 2, 1, 1)
     high_north, low_north = load_maps(2, 3, 1, 2), load_maps(0, 3, 1, 3)
     high_low, low_low = load_maps(2, 0, 2, 4), load_maps(0, 0, 2, 5)
-    for copy in load_traces + [high_east] + east_sources + [low_east, high_north] + north_sources + [low_north]:
-        copy.start()
-    for copy in [high_low] + low_sources + [low_low]:
+    for copy in [high_east] + load_traces + east_sources + [low_east, high_north] + north_sources + [low_north]:
         copy.start()
 
     barrier = pltpu.get_barrier_semaphore()
@@ -107,6 +105,8 @@
 
     def cols(k):
         return slice(k * face, (k + 1) * face)
+
+    later = [high_low] + low_sources + [low_low]
 
     for k, put_face, high_copy, low_copy, source_copies in (
         (2, put_east, high_east, low_east, east_sources),
@@ -126,6 +126,9 @@
             return carry
 
         lax.fori_loop(0, CHUNKS, first, 0)
+        if k == 2:
+            for copy in later:
+                copy.start()
 
     clear(recv_x, has_left, 0, turn)
     clear(recv_y, has_below, 0, turn)

time: 51.7 us -> 50.6 us (0.979)
  Pallas kernels: 48.5 us -> 47.3 us
    pallas_call x1, Pallas kernels: 48.5 us -> 47.3 us  [on_device(): pl.pallas_call(sweep, out_shape=jax.ShapeDtypeStruct(traces.shape, jnp.bf...]
where the time goes in v3:
time: 50.6 us; the launch traced here: 49.6 us
  Pallas kernels  47.3 us (93%)
  local copies, waits for them, and re-layouts  2.3 us (5%)
    pallas_call x1, Pallas kernels, on_device(): pl.pallas_call(sweep, out_shape=jax.ShapeDtypeStruct(traces.shape, jnp.bf...  47.3 us
    unnamed x1, local copies, waits for them, and re-layouts  2.3 us

profile of v3, /device:TPU:17, one launch (start us, length us, event | category | flops | bytes accessed | tf_op | source)
XLA Modules:
  0.0 49.6 jit_solution(6134922776992782498)
XLA Ops:
  0.0 47.3 %shard_map.37 = bf16[1,1,256,2048]{3,2,1,0:T(8,128)(2,1)} custom-call(bf16[1,1,2048,2048]{3,2,1,0:T(8,128)(2,1)} %maps_hbm.1, f32[1,1,256,2048]{3,2,1,0:T(8,128)} %sources_hbm.1, bf16[1,1,256,2048]{3,2,1,0:T(8,128)(2,1)} %traces_hbm.1), custom_call_target="tpu_custom_call" | custom-call | tf_op jit(solution)/shard_map/pallas_call | solution.py:242
  47.3 2.3 %copy.5 = bf16[1,1,256,2048]{3,2,1,0:T(8,128)(2,1)} copy(bf16[1,1,256,2048]{3,2,1,0:T(8,128)(2,1)} %shard_map.37) | data formatting | bytes 2097152
